TPU v7x, 32 devices: a whole 2x2x4 slice. The times are simulated.
32 devices in a mesh: groups: 2 (over x), seq: 16 (over z, y, core).
Axes of the slice: x: 2, y: 2, z: 4, core: 2. Of those that a mesh axis runs over, the one named last changes fastest.
Arguments:
- query_rows: bfloat16 [1536, 4096], P(('groups', 'seq')), parts along dimension 0, may hold values from -160 to 160
- key_rows: bfloat16 [1536, 4096], P(('groups', 'seq')), parts along dimension 0, may hold values from -8 to 8
- value_rows: bfloat16 [1536, 4096], P(('groups', 'seq')), parts along dimension 0, may hold values from -6 to 6
- proj_weight: bfloat16 [4096, 128], replicated, may hold values from -0.09375 to 0.09375
- in_weight: bfloat16 [3, 3, 3, 128, 512], replicated, may hold values from -0.109375 to 0.109375
- in_bias: float32 [512], replicated, may hold values from -3 to 3
- mid_weight: bfloat16 [3, 3, 3, 512, 512], P(None, None, None, None, 'seq'), may hold values from -0.0546875 to 0.0546875
- mid_bias: float32 [512], replicated, may hold values from -3 to 3
Outputs:
- upsampled: bfloat16 [32, 2, 2, 48, 128], P(('groups', 'seq')), parts along dimension 0
There are 2 independent parts, one for each index of `groups`. A program takes and returns all parts, laid end to end along the dimension named above; an argument that names none is the same for every part. Nothing has to cross between parts.
All inputs are finite; a program needn't handle non-finite values.
Results may differ from a plain program's by a relative error of at most 0.01.
Values may be sent and summed in bfloat16 or wider, within the bound.
No kernel may reach another device: no remote copies, remote signals or barrier semaphores. Data moves between devices by JAX's collectives and lax.ppermute only.
A program may use at most 128 MiB of HBM per device.

v0:
```python
import math

import jax
import jax.numpy as jnp
from jax import lax
from jax.sharding import PartitionSpec as P

D = 4096
HEADS = 32
HD = 128
C_LAT = 128
CH = 512
W = 24
F = 2
HT = 1


def padded_2(block, sides, width):
    for axis, dim in sides:
        count = lax.axis_size(axis)
        forward = [(i, i + 1) for i in range(count - 1)]
        backward = [(target, source) for source, target in forward]
        low = lax.ppermute(
            lax.slice_in_dim(block, block.shape[dim] - width, None, axis=dim), axis, forward
        )
        high = lax.ppermute(lax.slice_in_dim(block, 0, width, axis=dim), axis, backward)
        block = jnp.concatenate([low, block, high], axis=dim)
    return block


def unfold(padded, frames, height, columns):
    pieces = [
        padded[
            frame_off : frame_off + frames, row_off : row_off + height, col_off : col_off + columns
        ]
        for frame_off in range(3)
        for row_off in range(3)
        for col_off in range(3)
    ]
    return jnp.concatenate(pieces, axis=-1).reshape(frames * height * columns, -1)


def normed_latents(token_rows, proj_weight):
    widened = token_rows.astype(jnp.float32)
    normed = (
        widened * lax.rsqrt(jnp.mean(widened * widened, axis=1, keepdims=True) + 1e-06)
    ).astype(jnp.bfloat16)
    return jnp.dot(normed, proj_weight, preferred_element_type=jnp.float32).astype(jnp.bfloat16)


def extend(tile_cells):
    bordered = padded_2(tile_cells, (("seq", 1),), 1)
    return jnp.pad(bordered, ((1, 1), (0, 0), (1, 1), (0, 0)))


def shuffle_tile(summed, frames, height, columns):
    channels = summed.shape[-1] // 4
    return (
        summed.reshape(frames, height, columns, channels, 2, 2)
        .transpose(0, 1, 4, 2, 5, 3)
        .reshape(frames, 2 * height, 2 * columns, channels)
    )


def on_device(
    query_rows, key_rows, value_rows, proj_weight, in_weight, in_bias, mid_weight, mid_bias
):
    devices = lax.axis_size("seq")
    halves = max(1, devices // HEADS)
    unit_count = HEADS * halves // devices
    local_tokens = query_rows.shape[0]
    shard_rows = local_tokens // W
    half_width = W // halves
    score_scale = 1.0 / math.sqrt(HD)

    def by_head(rows):
        shaped = rows.reshape(local_tokens, HEADS, HD).transpose(1, 0, 2)
        shaped = jnp.broadcast_to(shaped[:, None], (HEADS, halves, local_tokens, HD))
        return shaped.reshape(devices, unit_count, local_tokens, HD)

    shaped = query_rows.reshape(shard_rows, halves, half_width, HEADS, HD).transpose(3, 1, 0, 2, 4)
    query_units = lax.all_to_all(
        shaped.reshape(devices, unit_count, shard_rows, half_width, HD),
        "seq",
        split_axis=0,
        concat_axis=0,
        tiled=True,
    )
    key_units = lax.all_to_all(by_head(key_rows), "seq", split_axis=0, concat_axis=0, tiled=True)
    value_units = lax.all_to_all(
        by_head(value_rows), "seq", split_axis=0, concat_axis=0, tiled=True
    )
    key_heads = key_units.transpose(1, 0, 2, 3).reshape(unit_count, -1, HD)
    value_heads = value_units.transpose(1, 0, 2, 3).reshape(unit_count, -1, HD)
    query_total = devices * shard_rows * half_width
    block_rows = 512 if query_total % 512 == 0 else query_total
    query_heads = (
        query_units.transpose(1, 0, 2, 3, 4)
        .reshape(unit_count, query_total // block_rows, block_rows, HD)
        .transpose(1, 0, 2, 3)
    )

    def attend(query_block):
        scores = (
            jnp.einsum("uqd,ukd->uqk", query_block, key_heads, preferred_element_type=jnp.float32)
            * score_scale
        )
        largest = jnp.max(scores, axis=2, keepdims=True)
        weights = jnp.exp(scores - largest)
        totals = jnp.sum(weights, axis=2, keepdims=True)
        mixture = jnp.einsum(
            "uqk,ukd->uqd",
            weights.astype(jnp.bfloat16),
            value_heads,
            preferred_element_type=jnp.float32,
        )
        return (mixture / totals).astype(jnp.bfloat16)

    attended = lax.map(attend, query_heads)
    attended = attended.transpose(1, 0, 2, 3).reshape(
        unit_count, devices, shard_rows, half_width, HD
    )
    arranged = attended.reshape(unit_count, F, devices, HT, half_width, HD).transpose(
        2, 0, 1, 3, 4, 5
    )
    arrived = lax.all_to_all(arranged, "seq", split_axis=0, concat_axis=0, tiled=True)
    arrived = arrived.reshape(HEADS, halves, F, HT, half_width, HD).transpose(2, 3, 1, 4, 0, 5)
    latents = normed_latents(arrived.reshape(F * HT * W, D), proj_weight).reshape(F, HT, W, C_LAT)
    unfolded_in = unfold(extend(latents), F, HT, W)
    first = (
        jnp.dot(unfolded_in, in_weight.reshape(27 * C_LAT, CH), preferred_element_type=jnp.float32)
        + in_bias
    ).astype(jnp.bfloat16)
    active = jax.nn.silu(first.astype(jnp.float32)).astype(jnp.bfloat16)
    unfolded_mid = unfold(extend(active.reshape(F, HT, W, CH)), F, HT, W)
    piece = lax.all_gather(mid_weight, "seq", axis=4, tiled=True)
    column_span = piece.shape[4]
    middle = (
        jnp.dot(
            unfolded_mid, piece.reshape(27 * CH, column_span), preferred_element_type=jnp.float32
        )
        + mid_bias
    ).astype(jnp.bfloat16)
    summed = first.astype(jnp.float32) + middle.astype(jnp.float32)
    return shuffle_tile(summed, F, HT, W).astype(jnp.bfloat16)[None]


def solution(mesh):
    return jax.shard_map(
        on_device,
        mesh=mesh,
        in_specs=(
            P(("groups", "seq"), None),
            P(("groups", "seq"), None),
            P(("groups", "seq"), None),
            P(),
            P(),
            P(),
            P(None, None, None, None, "seq"),
            P(),
        ),
        out_specs=P(("groups", "seq"), None, None, None, None),
        check_vma=False,
    )
```

profile of v0, /device:TPU:16, one launch (start us, length us, event | category | flops | bytes accessed | tf_op | source)
XLA Modules:
  0.0 199.5 jit_solution(9483234338959836332)
XLA Ops:
  6.5 0.7 all-gather.2.cloned.1.call-update
  7.3 1.4 copy.45
  8.7 0.9 copy.31
  9.6 6.2 %all-to-all-start = ((bf16[16,2,2,24,128]{4,3,2,1,0:T(8,128)(2,1)}), bf16[16,2,2,24,128]{4,3,2,1,0:T(8,128)(2,1)}, u32[]{:S(2)}, u32[]{:S(2)}) async-start(bf16[16,2,2,24,128]{4,3,2,1,0:T(8,128)(2,1)} %bitcast.118), calls=%async_computation | async-start | bytes 786432 | tf_op jit(solution)/shard_map/all_to_all | solution.py:82
  15.8 1.1 copy.46
  16.8 0.9 copy.33
  17.8 18.3 %all-to-all-done = bf16[16,2,2,24,128]{4,3,2,1,0:T(8,128)(2,1)} async-done(((bf16[16,2,2,24,128]{4,3,2,1,0:T(8,128)(2,1)}), bf16[16,2,2,24,128]{4,3,2,1,0:T(8,128)(2,1)}, u32[]{:S(2)}, u32[]{:S(2)}) %all-to-all-start) | async-done | bytes 393248 | tf_op jit(solution)/shard_map/all_to_all | solution.py:82
  36.1 4.7 %all-to-all-start.1 = ((bf16[16,2,48,128]{3,2,1,0:T(8,128)(2,1)}), bf16[16,2,48,128]{3,2,1,0:T(8,128)(2,1)}, u32[]{:S(2)}, u32[]{:S(2)}) async-start(bf16[16,2,48,128]{3,2,1,0:T(8,128)(2,1)} %bitcast.115), calls=%async_computation.1 | async-start | bytes 786432 | tf_op jit(solution)/shard_map/all_to_all | solution.py:89
  40.8 1.1 copy.47
  41.9 0.9 copy.35
  42.8 18.6 %all-to-all-done.1 = bf16[16,2,48,128]{3,2,1,0:T(8,128)(2,1)} async-done(((bf16[16,2,48,128]{3,2,1,0:T(8,128)(2,1)}), bf16[16,2,48,128]{3,2,1,0:T(8,128)(2,1)}, u32[]{:S(2)}, u32[]{:S(2)}) %all-to-all-start.1) | async-done | bytes 393248 | tf_op jit(solution)/shard_map/all_to_all | solution.py:89
  61.3 4.7 %all-to-all-start.2 = ((bf16[16,2,48,128]{3,2,1,0:T(8,128)(2,1)}), bf16[16,2,48,128]{3,2,1,0:T(8,128)(2,1)}, u32[]{:S(2)}, u32[]{:S(2)}) async-start(bf16[16,2,48,128]{3,2,1,0:T(8,128)(2,1)} %bitcast.114), calls=%async_computation.2 | async-start | bytes 786432 | tf_op jit(solution)/shard_map/all_to_all | solution.py:90
  66.0 1.8 copy.32
  67.8 1.8 copy.34
  69.5 18.4 %all-to-all-done.2 = bf16[16,2,48,128]{3,2,1,0:T(8,128)(2,1)} async-done(((bf16[16,2,48,128]{3,2,1,0:T(8,128)(2,1)}), bf16[16,2,48,128]{3,2,1,0:T(8,128)(2,1)}, u32[]{:S(2)}, u32[]{:S(2)}) %all-to-all-start.2) | async-done | bytes 393248 | tf_op jit(solution)/shard_map/all_to_all | solution.py:90
  87.9 1.0 copy.36
  88.9 1.9 multiply_reduce_fusion
  90.8 0.8 fusion
  91.6 1.3 fusion.15
  93.0 25.8 %all_to_all.20 = bf16[16,2,2,1,24,128]{5,4,2,1,3,0:T(8,128)(2,1)S(1)} all-to-all(bf16[16,2,2,1,24,128]{5,4,2,1,3,0:T(8,128)(2,1)S(1)} %bitcast.119), channel_id=1, replica_groups=mesh['groups'=2,'seq'=16] {'seq'}, dimensions={0} | all-to-all | bytes 786432 | tf_op jit(solution)/shard_map/all_to_all | solution.py:126
  118.8 0.7 copy-done.1
  119.8 1.2 bitcast_convert_fusion
  121.9 4.0 %collective-permute-start.1 = (bf16[2,1,24,128]{3,2,0,1:T(8,128)(2,1)S(1)}, bf16[2,1,24,128]{3,2,0,1:T(8,128)(2,1)S(1)}, u32[]{:S(2)}, u32[]{:S(2)}) collective-permute-start(bf16[2,1,24,128]{3,2,0,1:T(8,128)(2,1)S(1)} %bitcast.158), channel_id=1, source_target_pairs={{1,0},{2,1},{3,2},{4,3},{5,4},{6,5},{7,6},{8,7},{9,8},{10,9},{11,1... | collective-permute-start | bytes 36872 | tf_op jit(solution)/shard_map/ppermute | solution.py:26
  125.9 1.9 collective-permute-start
  127.8 4.4 %collective-permute-done = bf16[2,1,24,128]{3,2,0,1:T(8,128)(2,1)S(1)} collective-permute-done((bf16[2,1,24,128]{3,2,0,1:T(8,128)(2,1)S(1)}, bf16[2,1,24,128]{3,2,0,1:T(8,128)(2,1)S(1)}, u32[]{:S(2)}, u32[]{:S(2)}) %collective-permute-start) | collective-permute-done | bytes 12320 | tf_op jit(solution)/shard_map/ppermute | solution.py:23
  132.7 1.4 multiply_convert_fusion
  134.1 1.9 collective-permute-start.3
  136.0 2.4 %collective-permute-start.2 = (bf16[2,1,24,512]{3,2,0,1:T(8,128)(2,1)S(1)}, bf16[2,1,24,512]{3,2,0,1:T(8,128)(2,1)S(1)}, u32[]{:S(2)}, u32[]{:S(2)}) collective-permute-start(bf16[2,1,24,512]{3,2,0,1:T(8,128)(2,1)S(1)} %bitcast.125), channel_id=1, source_target_pairs={{0,1},{1,2},{2,3},{3,4},{4,5},{5,6},{6,7},{7,8},{8,9},{9,10},{10,1... | collective-permute-start | bytes 147464 | tf_op jit(solution)/shard_map/ppermute | solution.py:23
  138.7 4.5 %collective-permute-done.2 = bf16[2,1,24,512]{3,2,0,1:T(8,128)(2,1)S(1)} collective-permute-done((bf16[2,1,24,512]{3,2,0,1:T(8,128)(2,1)S(1)}, bf16[2,1,24,512]{3,2,0,1:T(8,128)(2,1)S(1)}, u32[]{:S(2)}, u32[]{:S(2)}) %collective-permute-start.2) | collective-permute-done | bytes 49184 | tf_op jit(solution)/shard_map/ppermute | solution.py:23
  143.3 0.6 constant_dynamic-update-slice_fusion.53
  144.0 0.6 constant_dynamic-update-slice_fusion.52
  145.2 0.7 constant_dynamic-update-slice_fusion.50
  146.6 0.6 constant_dynamic-update-slice_fusion.48
  147.3 0.6 constant_dynamic-update-slice_fusion.47
  147.9 0.6 constant_dynamic-update-slice_fusion.46
  148.5 0.6 constant_dynamic-update-slice_fusion.45
  149.1 0.7 constant_dynamic-update-slice_fusion.44
  149.8 0.6 constant_dynamic-update-slice_fusion.43
  152.3 0.6 constant_dynamic-update-slice_fusion.39
  156.6 0.6 constant_dynamic-update-slice_fusion.32
  157.2 0.6 constant_dynamic-update-slice_fusion.31
  159.1 0.6 constant_dynamic-update-slice_fusion.28
  159.8 0.6 constant_dynamic-update-slice_fusion.27
  160.4 18.7 %copy.41 = bf16[3,3,3,512,512]{4,3,2,1,0:T(8,128)(2,1)} copy(bf16[3,3,3,512,512]{3,4,2,1,0:T(8,128)(2,1)} %all-gather.2.cloned.1.call-done) | data formatting | bytes 28311552 | tf_op jit(solution)/shard_map/all_gather | solution.py:136
  179.1 8.5 %fusion.11 = bf16[48,512]{1,0:T(8,128)(2,1)} fusion(f32[48,512]{1,0:T(8,128)} %get-tuple-element.71, bf16[48,13824]{1,0:T(8,128)(2,1)} %constant_dynamic-update-slice_fusion.27, bf16[13824,512]{1,0:T(8,128)(2,1)} %bitcast.111, f32[512]{0:T(512)S(1)} %copy-done.4), kind=kOutput, calls=%fused_computation.18 | convolution fusion | flops 679600128 | bytes 15632384 | tf_op jit(solution)/shard_map/dot_general | solution.py:139
  187.6 1.6 copy.42
  189.1 1.7 convert_element_type.85
  190.9 1.8 copy.43
  (65 shorter events, 10.1 us)
Async XLA Ops:
  6.5 126.1 %copy-start = (bf16[3,3,3,128,512]{4,3,2,1,0:T(8,128)(2,1)S(1)}, bf16[3,3,3,128,512]{4,3,2,1,0:T(8,128)(2,1)}, u32[]{:S(2)}) copy-start(bf16[3,3,3,128,512]{4,3,2,1,0:T(8,128)(2,1)} %param.12) | copy-start | bytes 10616836
  6.5 153.9 %all-gather.2.cloned.1.call-start = ((), (), s32[]{:S(2)}) async-start(), calls=%async_computation.4 | async-start | bytes 15040512 | tf_op jit(solution)/shard_map/all_gather | solution.py:136
  9.6 26.5 %all-to-all-start = ((bf16[16,2,2,24,128]{4,3,2,1,0:T(8,128)(2,1)}), bf16[16,2,2,24,128]{4,3,2,1,0:T(8,128)(2,1)}, u32[]{:S(2)}, u32[]{:S(2)}) async-start(bf16[16,2,2,24,128]{4,3,2,1,0:T(8,128)(2,1)} %bitcast.118), calls=%async_computation | async-start | bytes 786432 | tf_op jit(solution)/shard_map/all_to_all | solution.py:82
  36.1 25.2 %all-to-all-start.1 = ((bf16[16,2,48,128]{3,2,1,0:T(8,128)(2,1)}), bf16[16,2,48,128]{3,2,1,0:T(8,128)(2,1)}, u32[]{:S(2)}, u32[]{:S(2)}) async-start(bf16[16,2,48,128]{3,2,1,0:T(8,128)(2,1)} %bitcast.115), calls=%async_computation.1 | async-start | bytes 786432 | tf_op jit(solution)/shard_map/all_to_all | solution.py:89
  61.3 26.5 %all-to-all-start.2 = ((bf16[16,2,48,128]{3,2,1,0:T(8,128)(2,1)}), bf16[16,2,48,128]{3,2,1,0:T(8,128)(2,1)}, u32[]{:S(2)}, u32[]{:S(2)}) async-start(bf16[16,2,48,128]{3,2,1,0:T(8,128)(2,1)} %bitcast.114), calls=%async_computation.2 | async-start | bytes 786432 | tf_op jit(solution)/shard_map/all_to_all | solution.py:90
  118.8 0.7 copy-start.1
  119.8 1.5 copy-start.2
  121.2 11.4 %copy-start.3 = (f32[512]{0:T(512)S(1)}, f32[512]{0:T(512)}, u32[]{:S(2)}) copy-start(f32[512]{0:T(512)} %param.13) | copy-start | bytes 6148
  121.9 6.0 %collective-permute-start.1 = (bf16[2,1,24,128]{3,2,0,1:T(8,128)(2,1)S(1)}, bf16[2,1,24,128]{3,2,0,1:T(8,128)(2,1)S(1)}, u32[]{:S(2)}, u32[]{:S(2)}) collective-permute-start(bf16[2,1,24,128]{3,2,0,1:T(8,128)(2,1)S(1)} %bitcast.158), channel_id=1, source_target_pairs={{1,0},{2,1},{3,2},{4,3},{5,4},{6,5},{7,6},{8,7},{9,8},{10,9},{11,1... | collective-permute-start | bytes 36872 | tf_op jit(solution)/shard_map/ppermute | solution.py:26
  125.9 6.3 %collective-permute-start = (bf16[2,1,24,128]{3,2,0,1:T(8,128)(2,1)S(1)}, bf16[2,1,24,128]{3,2,0,1:T(8,128)(2,1)S(1)}, u32[]{:S(2)}, u32[]{:S(2)}) collective-permute-start(bf16[2,1,24,128]{3,2,0,1:T(8,128)(2,1)S(1)} %bitcast.159), channel_id=1, source_target_pairs={{0,1},{1,2},{2,3},{3,4},{4,5},{5,6},{6,7},{7,8},{8,9},{9,10},{10,1... | collective-permute-start | bytes 36872 | tf_op jit(solution)/shard_map/ppermute | solution.py:23
  134.1 4.7 %collective-permute-start.3 = (bf16[2,1,24,512]{3,2,0,1:T(8,128)(2,1)S(1)}, bf16[2,1,24,512]{3,2,0,1:T(8,128)(2,1)S(1)}, u32[]{:S(2)}, u32[]{:S(2)}) collective-permute-start(bf16[2,1,24,512]{3,2,0,1:T(8,128)(2,1)S(1)} %bitcast.124), channel_id=1, source_target_pairs={{1,0},{2,1},{3,2},{4,3},{5,4},{6,5},{7,6},{8,7},{9,8},{10,9},{11,1... | collective-permute-start | bytes 147464 | tf_op jit(solution)/shard_map/ppermute | solution.py:26
  136.0 7.2 %collective-permute-start.2 = (bf16[2,1,24,512]{3,2,0,1:T(8,128)(2,1)S(1)}, bf16[2,1,24,512]{3,2,0,1:T(8,128)(2,1)S(1)}, u32[]{:S(2)}, u32[]{:S(2)}) collective-permute-start(bf16[2,1,24,512]{3,2,0,1:T(8,128)(2,1)S(1)} %bitcast.125), channel_id=1, source_target_pairs={{0,1},{1,2},{2,3},{3,4},{4,5},{5,6},{6,7},{7,8},{8,9},{9,10},{10,1... | collective-permute-start | bytes 147464 | tf_op jit(solution)/shard_map/ppermute | solution.py:23
  160.4 18.7 %copy-start.4 = (f32[512]{0:T(512)S(1)}, f32[512]{0:T(512)}, u32[]{:S(2)}) copy-start(f32[512]{0:T(512)} %param.15) | copy-start | bytes 6148
Sparse Core Ops, SparseCore 0:
  9.5 131.9 all-gather.1
where the time goes:
time: 201 us; the launch traced here: 199 us
  waiting for transfers between devices  65.1 us (32%)
  local copies, waits for them, and re-layouts  53.1 us (26%)
  starting transfers between devices  25.8 us (13%)
  blocking collectives  25.8 us (13%)
  matrix products  13.7 us (7%)
  between operations  13.7 us (7%)
  other arithmetic  2.23 us (1%)
    all_to_all x1, blocking collectives, on_device(): lax.all_to_all(arranged, 'seq', split_axis=0, concat_axis=0, tiled=True)  25.8 us
    unnamed x65, local copies, waits for them, and re-layouts  20.8 us
    all_gather x1, local copies, waits for them, and re-layouts, on_device(): piece = lax.all_gather(mid_weight, 'seq', axis=4, tiled=True)  18.7 us
    all_to_all x1, waiting for transfers between devices, on_device(): lax.all_to_all(by_head(key_rows), 'seq', split_axis=0, concat_axis=0, til...  18.6 us
    all_to_all x1, waiting for transfers between devices, on_device(): lax.all_to_all(by_head(value_rows), 'seq', split_axis=0, concat_axis=0, t...  18.4 us
    all_to_all x1, waiting for transfers between devices, on_device(): lax.all_to_all(shaped.reshape(devices, unit_count, shard_rows, half_width...  18.3 us
    ppermute x2, waiting for transfers between devices, padded_2(): lax.ppermute(lax.slice_in_dim(block, block.shape[dim] - width, None, axis...  8.83 us
    dot_general x1, matrix products, on_device(): jnp.dot(unfolded_mid, piece.reshape(27 * CH, column_span), preferred_elem...  8.49 us
  transfers between devices with their start and end apart: 8, of which 6 were waited for; matrix products, arithmetic and copies ran while one was open for 18% of the time, Pallas kernels for 0%

commit v1 on v0

--- a/solution.py
+++ b/solution.py
@@ -3,6 +3,8 @@
 import jax
 import jax.numpy as jnp
 from jax import lax
+from jax.experimental import pallas as pl
+from jax.experimental.pallas import tpu as pltpu
 from jax.sharding import PartitionSpec as P
 
 D = 4096
@@ -62,7 +64,7 @@
     )
 
 
-def on_device(
+def shared_heads(
     query_rows, key_rows, value_rows, proj_weight, in_weight, in_bias, mid_weight, mid_bias
 ):
     devices = lax.axis_size("seq")
@@ -143,6 +145,230 @@
     ).astype(jnp.bfloat16)
     summed = first.astype(jnp.float32) + middle.astype(jnp.float32)
     return shuffle_tile(summed, F, HT, W).astype(jnp.bfloat16)[None]
+
+
+def dot_f32(left, right, left_dim=1, right_dim=0):
+    return lax.dot_general(
+        left, right, (((left_dim,), (right_dim,)), ((), ())), preferred_element_type=jnp.float32
+    )
+
+
+def pack_body(query_ref, key_ref, value_ref, out_ref):
+    devices, _, _, span = out_ref.shape
+    for which, ref in enumerate((query_ref, key_ref, value_ref)):
+        for target in range(devices):
+            out_ref[target, which] = ref[:, target * span : (target + 1) * span]
+
+
+def attend_body(rank_ref, rows_ref, proj_ref, out_ref, proj_buf, proj_sem):
+    devices, _, local, span = rows_ref.shape
+    tokens = devices * local
+    start = pl.multiple_of(rank_ref[0] * span, span)
+    copy = pltpu.make_async_copy(proj_ref.at[pl.ds(start, span), :], proj_buf, proj_sem)
+    copy.start()
+    query = rows_ref[:, 0].reshape(tokens, span)
+    key = rows_ref[:, 1].reshape(tokens, span)
+    value = rows_ref[:, 2].reshape(tokens, span)
+    score_scale = 1.0 / math.sqrt(HD)
+    heads = []
+    for unit in range(span // HD):
+        lanes = slice(unit * HD, (unit + 1) * HD)
+        scores = dot_f32(query[:, lanes], key[:, lanes], 1, 1) * score_scale
+        largest = jnp.max(scores, axis=1, keepdims=True)
+        weights = jnp.exp(scores - largest)
+        totals = jnp.sum(weights, axis=1, keepdims=True)
+        mixture = dot_f32(weights.astype(jnp.bfloat16), value[:, lanes])
+        heads.append((mixture / totals).astype(jnp.bfloat16))
+    attended = jnp.concatenate(heads, axis=1)
+    widened = attended.astype(jnp.float32)
+    squares = jnp.sum(widened * widened, axis=1, keepdims=True)
+    copy.wait()
+    partial = dot_f32(attended, proj_buf[...])
+    out_ref[:, :local, :] = partial.reshape(devices, local, C_LAT).astype(jnp.bfloat16)
+    lane = lax.broadcasted_iota(jnp.int32, (devices, local, C_LAT), 2)
+    row = lax.broadcasted_iota(jnp.int32, (devices, local, C_LAT), 1)
+    spread = jnp.broadcast_to(squares, (tokens, C_LAT)).reshape(devices, local, C_LAT)
+    across = jnp.sum(jnp.where(lane == row, spread, 0.0), axis=1, keepdims=True)
+    coarse = across.astype(jnp.bfloat16).astype(jnp.float32)
+    extra = out_ref.shape[1] - local
+    line = lax.broadcasted_iota(jnp.int32, (devices, extra, C_LAT), 1)
+    tail = jnp.where(line == 0, coarse, jnp.where(line == 1, across - coarse, 0.0))
+    out_ref[:, local:, :] = tail.astype(jnp.bfloat16)
+
+
+def latents_body(parts_ref, out_ref):
+    devices, local, _ = out_ref.shape
+    total = jnp.sum(parts_ref[:, :local, :].astype(jnp.float32), axis=0)
+    tail = jnp.sum(parts_ref[:, local:, :].astype(jnp.float32), axis=0)
+    across = tail[0:1] + tail[1:2]
+    lane = lax.broadcasted_iota(jnp.int32, (local, C_LAT), 1)
+    row = lax.broadcasted_iota(jnp.int32, (local, C_LAT), 0)
+    squares = jnp.sum(jnp.where(lane == row, across, 0.0), axis=1, keepdims=True)
+    latents = (total * lax.rsqrt(squares / D + 1e-06)).astype(jnp.bfloat16)
+    for target in range(devices):
+        out_ref[target] = latents
+
+
+def convolve_body(
+    rank_ref, latents_ref, in_weight_ref, in_bias_ref, mid_weight_ref, mid_bias_ref, out_ref, cols
+):
+    frame = latents_ref.shape[0] // F
+    own = mid_weight_ref.shape[1] // 9
+    column = lax.broadcasted_iota(jnp.int32, (frame, C_LAT), 0) % W
+    for index in range(F):
+        cells = latents_ref[index * frame : (index + 1) * frame, :].astype(jnp.float32)
+        shifted = (
+            jnp.where(column == 0, 0.0, pltpu.roll(cells, 1, 0)),
+            cells,
+            jnp.where(column == W - 1, 0.0, pltpu.roll(cells, frame - 1, 0)),
+        )
+        blank = jnp.zeros((W, C_LAT), jnp.float32)
+        for col_off, moved in enumerate(shifted):
+            above = jnp.concatenate([blank, moved[:-W]], axis=0)
+            below = jnp.concatenate([moved[W:], blank], axis=0)
+            for row_off, piece in enumerate((above, moved, below)):
+                at = ((index * 3 + row_off) * 3 + col_off) * C_LAT
+                cols[:, at : at + C_LAT] = piece.astype(jnp.bfloat16)
+    deep = 9 * C_LAT
+    firsts = []
+    actives = []
+    for index in range(F):
+        low = (F - 1 - index) * deep
+        first = (
+            dot_f32(cols[...], in_weight_ref[low : low + F * deep, :]) + in_bias_ref[...]
+        ).astype(jnp.bfloat16)
+        wide = first.astype(jnp.float32)
+        firsts.append(first)
+        actives.append((wide / (1.0 + jnp.exp(-wide))).astype(jnp.bfloat16))
+    channel = lax.broadcasted_iota(jnp.int32, (own, CH), 1)
+    mine = channel == lax.broadcasted_iota(jnp.int32, (own, CH), 0) + rank_ref[0] * own
+    bias = jnp.sum(jnp.where(mine, mid_bias_ref[...], 0.0), axis=1, keepdims=True)
+    chosen = jnp.where(mine, 1.0, 0.0).astype(jnp.bfloat16)
+    spot = lax.broadcasted_iota(jnp.int32, (own, frame), 1)
+    spot_column = spot % W
+    outs = []
+    for index in range(F):
+        taps = sum(
+            dot_f32(mid_weight_ref[source - index + 1], actives[source], 1, 1)
+            for source in range(F)
+        )
+        total = None
+        for col_off in range(3):
+            merged = None
+            for row_off in range(3):
+                at = (row_off * 3 + col_off) * own
+                piece = taps[at : at + own, :]
+                if row_off == 0:
+                    piece = jnp.where(spot < W, 0.0, pltpu.roll(piece, W, 1))
+                elif row_off == 2:
+                    piece = jnp.where(spot >= frame - W, 0.0, pltpu.roll(piece, frame - W, 1))
+                merged = piece if merged is None else merged + piece
+            if col_off == 0:
+                merged = jnp.where(spot_column == 0, 0.0, pltpu.roll(merged, 1, 1))
+            elif col_off == 2:
+                merged = jnp.where(spot_column == W - 1, 0.0, pltpu.roll(merged, frame - 1, 1))
+            total = merged if total is None else total + merged
+        middle = (total + bias).astype(jnp.bfloat16).astype(jnp.float32)
+        outs.append((dot_f32(chosen, firsts[index], 1, 1) + middle).astype(jnp.bfloat16))
+    stacked = jnp.concatenate(outs, axis=0)
+    source = lax.broadcasted_iota(jnp.int32, (F * own, 128), 0)
+    target = lax.broadcasted_iota(jnp.int32, (F * own, 128), 1)
+    inner = source % own
+    place = (source // own) * own + (inner % 4) * (own // 4) + inner // 4
+    moves = jnp.where(place == target, 1.0, 0.0).astype(jnp.bfloat16)
+    out_ref[...] = dot_f32(stacked, moves, 0, 0).astype(jnp.bfloat16)
+
+
+def shuffle_body(rows_ref, out_ref, wide):
+    devices = rows_ref.shape[0] // W
+    share = C_LAT // devices
+    rows = rows_ref[...].astype(jnp.float32)
+    lane = lax.broadcasted_iota(jnp.int32, (W, 128), 1) // share
+    for index in range(F):
+        for part in range(4):
+            origin = (index * 4 + part) * share
+            total = None
+            for source in range(devices):
+                block = rows[source * W : (source + 1) * W, :]
+                moved = pltpu.roll(block, (source * share - origin) % 128, 1)
+                total = moved if total is None else jnp.where(lane == source, moved, total)
+            wide[index, part // 2, pl.ds(part % 2, W, stride=2), :] = total
+    out_ref[0] = wide[...].astype(jnp.bfloat16)
+
+
+def vmem(count):
+    return [pl.BlockSpec(memory_space=pltpu.VMEM)] * count
+
+
+def exchange(blocks):
+    return lax.all_to_all(blocks, "seq", split_axis=0, concat_axis=0, tiled=True)
+
+
+def whole_heads(
+    query_rows, key_rows, value_rows, proj_weight, in_weight, in_bias, mid_weight, mid_bias
+):
+    devices = lax.axis_size("seq")
+    local = query_rows.shape[0]
+    span = D // devices
+    frame = devices * local // F
+    own = mid_weight.shape[4]
+    rank = lax.axis_index("seq").reshape(1).astype(jnp.int32)
+    scalar = pl.BlockSpec(memory_space=pltpu.SMEM)
+    packed = pl.pallas_call(
+        pack_body,
+        out_shape=jax.ShapeDtypeStruct((devices, 3, local, span), jnp.bfloat16),
+        in_specs=vmem(3),
+        out_specs=vmem(1)[0],
+        name="pack",
+    )(query_rows, key_rows, value_rows)
+    rows = exchange(packed)
+    parts = pl.pallas_call(
+        attend_body,
+        out_shape=jax.ShapeDtypeStruct((devices, local + 16, C_LAT), jnp.bfloat16),
+        in_specs=[scalar, vmem(1)[0], pl.BlockSpec(memory_space=pl.ANY)],
+        out_specs=vmem(1)[0],
+        scratch_shapes=[pltpu.VMEM((span, C_LAT), jnp.bfloat16), pltpu.SemaphoreType.DMA(())],
+        name="attend",
+    )(rank, rows, proj_weight)
+    parts = exchange(parts)
+    copies = pl.pallas_call(
+        latents_body,
+        out_shape=jax.ShapeDtypeStruct((devices, local, C_LAT), jnp.bfloat16),
+        in_specs=vmem(1),
+        out_specs=vmem(1)[0],
+        name="latents",
+    )(parts)
+    latents = exchange(copies).reshape(devices * local, C_LAT)
+    columns = pl.pallas_call(
+        convolve_body,
+        out_shape=jax.ShapeDtypeStruct((frame, 128), jnp.bfloat16),
+        in_specs=[scalar] + vmem(5),
+        out_specs=vmem(1)[0],
+        scratch_shapes=[pltpu.VMEM((frame, F * 9 * C_LAT), jnp.bfloat16)],
+        name="convolve",
+    )(
+        rank,
+        latents,
+        in_weight.reshape(27 * C_LAT, CH),
+        in_bias.reshape(1, CH),
+        mid_weight.transpose(0, 1, 2, 4, 3).reshape(3, 9 * own, CH),
+        mid_bias.reshape(1, CH),
+    )
+    landed = exchange(columns.reshape(devices, W, 128)).reshape(frame, 128)
+    return pl.pallas_call(
+        shuffle_body,
+        out_shape=jax.ShapeDtypeStruct((1, F, 2, 2 * W, C_LAT), jnp.bfloat16),
+        in_specs=vmem(1),
+        out_specs=vmem(1)[0],
+        scratch_shapes=[pltpu.VMEM((F, 2, 2 * W, C_LAT), jnp.float32)],
+        name="shuffle",
+    )(landed)
+
+
+def on_device(*operands):
+    if lax.axis_size("seq") > HEADS:
+        return shared_heads(*operands)
+    return whole_heads(*operands)
 
 
 def solution(mesh):

time: 201 us -> 93.2 us (0.46)
  the two profiles are of different devices: /device:TPU:16 before, /device:TPU:0 now
where the time goes in v1:
time: 93.2 us; the launch traced here: 92.6 us
  blocking collectives  42.2 us (45%)
  waiting for transfers between devices  25 us (27%)
  Pallas kernels  16.9 us (18%)
  starting transfers between devices  7.41 us (8%)
  local copies, waits for them, and re-layouts  1.02 us (1%)
    all_to_all x3, blocking collectives, exchange(): lax.all_to_all(blocks, 'seq', split_axis=0, concat_axis=0, tiled=True)  42.2 us
    all_to_all x1, waiting for transfers between devices, exchange(): lax.all_to_all(blocks, 'seq', split_axis=0, concat_axis=0, tiled=True)  25 us
    all_to_all x1, starting transfers between devices, exchange(): lax.all_to_all(blocks, 'seq', split_axis=0, concat_axis=0, tiled=True)  7.41 us
    pallas_call x1, Pallas kernels, whole_heads(): pl.pallas_call(convolve_body, out_shape=jax.ShapeDtypeStruct((frame, 128)...  6.28 us
    pallas_call x1, Pallas kernels, whole_heads(): pl.pallas_call(attend_body, out_shape=jax.ShapeDtypeStruct((devices, loca...  4.72 us
    pallas_call x1, Pallas kernels, whole_heads(): pl.pallas_call(pack_body, out_shape=jax.ShapeDtypeStruct((devices, 3, loc...  2.33 us
  transfers between devices with their start and end apart: 1, of which 1 were waited for; matrix products, arithmetic and copies ran while one was open for 0% of the time, Pallas kernels for 0%

profile of v1, /device:TPU:0, one launch (start us, length us, event | category | flops | bytes accessed | tf_op | source)
XLA Modules:
  0.0 92.6 jit_solution(3859600427792119034)
XLA Ops:
  0.0 2.3 %pack.1 = bf16[16,3,48,256]{3,2,1,0:T(8,128)(2,1)} custom-call(bf16[48,4096]{1,0:T(8,128)(2,1)} %query_ref.1, bf16[48,4096]{1,0:T(8,128)(2,1)} %key_ref.1, bf16[48,4096]{1,0:T(8,128)(2,1)} %value_ref.1), custom_call_target="tpu_custom_call" | custom-call | tf_op jit(solution)/shard_map/pack/pallas_call | solution.py:317
  2.3 7.4 %all-to-all-start = ((bf16[16,3,48,256]{3,2,1,0:T(8,128)(2,1)}), bf16[16,3,48,256]{3,2,1,0:T(8,128)(2,1)S(1)}, u32[]{:S(2)}, u32[]{:S(2)}) async-start(bf16[16,3,48,256]{3,2,1,0:T(8,128)(2,1)} %pack.1), calls=%async_computation | async-start | bytes 2359296 | tf_op jit(solution)/shard_map/all_to_all | solution.py:304
  9.8 25.0 %all-to-all-done.rows_ref = bf16[16,3,48,256]{3,2,1,0:T(8,128)(2,1)S(1)} async-done(((bf16[16,3,48,256]{3,2,1,0:T(8,128)(2,1)}), bf16[16,3,48,256]{3,2,1,0:T(8,128)(2,1)S(1)}, u32[]{:S(2)}, u32[]{:S(2)}) %all-to-all-start) | async-done | bytes 1179680 | tf_op jit(solution)/shard_map/all_to_all | solution.py:304
  34.8 0.0 copy-start
  34.8 1.0 %copy-done = bf16[16,3,48,256]{3,2,1,0:T(8,128)(2,1)} copy-done((bf16[16,3,48,256]{3,2,1,0:T(8,128)(2,1)}, bf16[16,3,48,256]{3,2,1,0:T(8,128)(2,1)S(1)}, u32[]{:S(2)}) %copy-start) | copy-done | bytes 1179672
  35.8 4.7 %attend.1 = bf16[16,64,128]{2,1,0:T(8,128)(2,1)} custom-call(s32[1]{0:T(128)} %bitcast.rank_ref, bf16[16,3,48,256]{3,2,1,0:T(8,128)(2,1)} %copy-done, bf16[4096,128]{1,0:T(8,128)(2,1)} %proj_ref.1), custom_call_target="tpu_custom_call" | custom-call | tf_op jit(solution)/shard_map/attend/pallas_call | solution.py:325
  40.5 17.6 %all_to_all.20.parts_ref = bf16[16,64,128]{2,1,0:T(8,128)(2,1)} all-to-all(bf16[16,64,128]{2,1,0:T(8,128)(2,1)} %attend.1), channel_id=1, replica_groups=mesh['groups'=2,'seq'=16] {'seq'}, dimensions={0} | all-to-all | bytes 524288 | tf_op jit(solution)/shard_map/all_to_all | solution.py:304
  58.1 1.8 %latents.1 = bf16[16,48,128]{2,1,0:T(8,128)(2,1)} custom-call(bf16[16,64,128]{2,1,0:T(8,128)(2,1)} %all_to_all.20.parts_ref), custom_call_target="tpu_custom_call" | custom-call | tf_op jit(solution)/shard_map/latents/pallas_call | solution.py:334
  59.9 13.1 %all_to_all.21 = bf16[16,48,128]{2,1,0:T(8,128)(2,1)} all-to-all(bf16[16,48,128]{2,1,0:T(8,128)(2,1)} %latents.1), channel_id=1, replica_groups=mesh['groups'=2,'seq'=16] {'seq'}, dimensions={0} | all-to-all | bytes 393216 | tf_op jit(solution)/shard_map/all_to_all | solution.py:304
  73.0 6.3 %convolve.1 = bf16[384,128]{1,0:T(8,128)(2,1)} custom-call(s32[1]{0:T(128)} %bitcast.rank_ref, bf16[768,128]{1,0:T(8,128)(2,1)} %bitcast.12, bf16[3456,512]{1,0:T(8,128)(2,1)} %bitcast.10, f32[1,512]{1,0:T(1,128)} %bitcast.15, bf16[3,288,512]{2,1,0:T(8,128)(2,1)} %bitcast.11, f32[1,512]{1,0:T(1,128)} %bitcast.16), custom_call_target="tpu_custom_call" | custom-call | tf_op jit(solution)/shard_map/convolve/pallas_call | solution.py:342
  79.3 11.5 %all_to_all.22 = bf16[16,24,128]{2,1,0:T(8,128)(2,1)} all-to-all(bf16[16,24,128]{2,1,0:T(8,128)(2,1)} %bitcast.14), channel_id=1, replica_groups=mesh['groups'=2,'seq'=16] {'seq'}, dimensions={0} | all-to-all | bytes 196608 | tf_op jit(solution)/shard_map/all_to_all | solution.py:304
  90.8 1.8 %shuffle.1 = bf16[1,2,2,48,128]{4,3,2,1,0:T(8,128)(2,1)} custom-call(bf16[384,128]{1,0:T(8,128)(2,1)} %bitcast.13), custom_call_target="tpu_custom_call" | custom-call | tf_op jit(solution)/shard_map/shuffle/pallas_call | solution.py:358
Async XLA Ops:
  2.3 32.5 %all-to-all-start = ((bf16[16,3,48,256]{3,2,1,0:T(8,128)(2,1)}), bf16[16,3,48,256]{3,2,1,0:T(8,128)(2,1)S(1)}, u32[]{:S(2)}, u32[]{:S(2)}) async-start(bf16[16,3,48,256]{3,2,1,0:T(8,128)(2,1)} %pack.1), calls=%async_computation | async-start | bytes 2359296 | tf_op jit(solution)/shard_map/all_to_all | solution.py:304
  34.8 1.0 %copy-start = (bf16[16,3,48,256]{3,2,1,0:T(8,128)(2,1)}, bf16[16,3,48,256]{3,2,1,0:T(8,128)(2,1)S(1)}, u32[]{:S(2)}) copy-start(bf16[16,3,48,256]{3,2,1,0:T(8,128)(2,1)S(1)} %all-to-all-done.rows_ref) | copy-start | bytes 3538948

commit v2 on v1

--- a/solution.py
+++ b/solution.py
@@ -153,11 +153,22 @@
     )
 
 
-def pack_body(query_ref, key_ref, value_ref, out_ref):
+def pack_body(query_ref, key_ref, value_ref, out_ref, sems):
     devices, _, _, span = out_ref.shape
-    for which, ref in enumerate((query_ref, key_ref, value_ref)):
-        for target in range(devices):
-            out_ref[target, which] = ref[:, target * span : (target + 1) * span]
+    copies = []
+    for target in range(devices):
+        for which, ref in enumerate((query_ref, key_ref, value_ref)):
+            copies.append(
+                pltpu.make_async_copy(
+                    ref.at[:, target * span : (target + 1) * span],
+                    out_ref.at[target, which],
+                    sems.at[target, which],
+                )
+            )
+    for copy in copies:
+        copy.start()
+    for copy in copies:
+        copy.wait()
 
 
 def attend_body(rank_ref, rows_ref, proj_ref, out_ref, proj_buf, proj_sem):
@@ -296,6 +307,10 @@
     out_ref[0] = wide[...].astype(jnp.bfloat16)
 
 
+def near(array):
+    return pltpu.with_memory_space_constraint(array, pltpu.VMEM)
+
+
 def vmem(count):
     return [pl.BlockSpec(memory_space=pltpu.VMEM)] * count
 
@@ -316,42 +331,47 @@
     scalar = pl.BlockSpec(memory_space=pltpu.SMEM)
     packed = pl.pallas_call(
         pack_body,
-        out_shape=jax.ShapeDtypeStruct((devices, 3, local, span), jnp.bfloat16),
-        in_specs=vmem(3),
+        out_shape=pltpu.VMEM((devices, 3, local, span), jnp.bfloat16),
+        in_specs=[pl.BlockSpec(memory_space=pl.ANY)] * 3,
         out_specs=vmem(1)[0],
+        scratch_shapes=[pltpu.SemaphoreType.DMA((devices, 3))],
+        compiler_params=pltpu.CompilerParams(vmem_limit_bytes=8 << 20),
         name="pack",
     )(query_rows, key_rows, value_rows)
     rows = exchange(packed)
     parts = pl.pallas_call(
         attend_body,
-        out_shape=jax.ShapeDtypeStruct((devices, local + 16, C_LAT), jnp.bfloat16),
+        out_shape=pltpu.VMEM((devices, local + 8, C_LAT), jnp.bfloat16),
         in_specs=[scalar, vmem(1)[0], pl.BlockSpec(memory_space=pl.ANY)],
         out_specs=vmem(1)[0],
         scratch_shapes=[pltpu.VMEM((span, C_LAT), jnp.bfloat16), pltpu.SemaphoreType.DMA(())],
+        compiler_params=pltpu.CompilerParams(vmem_limit_bytes=32 << 20),
         name="attend",
-    )(rank, rows, proj_weight)
+    )(rank, near(rows), proj_weight)
     parts = exchange(parts)
     copies = pl.pallas_call(
         latents_body,
-        out_shape=jax.ShapeDtypeStruct((devices, local, C_LAT), jnp.bfloat16),
+        out_shape=pltpu.VMEM((devices, local, C_LAT), jnp.bfloat16),
         in_specs=vmem(1),
         out_specs=vmem(1)[0],
+        compiler_params=pltpu.CompilerParams(vmem_limit_bytes=8 << 20),
         name="latents",
-    )(parts)
+    )(near(parts))
     latents = exchange(copies).reshape(devices * local, C_LAT)
     columns = pl.pallas_call(
         convolve_body,
-        out_shape=jax.ShapeDtypeStruct((frame, 128), jnp.bfloat16),
+        out_shape=pltpu.VMEM((frame, 128), jnp.bfloat16),
         in_specs=[scalar] + vmem(5),
         out_specs=vmem(1)[0],
         scratch_shapes=[pltpu.VMEM((frame, F * 9 * C_LAT), jnp.bfloat16)],
+        compiler_params=pltpu.CompilerParams(vmem_limit_bytes=32 << 20),
         name="convolve",
     )(
         rank,
-        latents,
-        in_weight.reshape(27 * C_LAT, CH),
+        near(latents),
+        near(in_weight.reshape(27 * C_LAT, CH)),
         in_bias.reshape(1, CH),
-        mid_weight.transpose(0, 1, 2, 4, 3).reshape(3, 9 * own, CH),
+        near(mid_weight.transpose(0, 1, 2, 4, 3).reshape(3, 9 * own, CH)),
         mid_bias.reshape(1, CH),
     )
     landed = exchange(columns.reshape(devices, W, 128)).reshape(frame, 128)
@@ -361,8 +381,9 @@
         in_specs=vmem(1),
         out_specs=vmem(1)[0],
         scratch_shapes=[pltpu.VMEM((F, 2, 2 * W, C_LAT), jnp.float32)],
+        compiler_params=pltpu.CompilerParams(vmem_limit_bytes=8 << 20),
         name="shuffle",
-    )(landed)
+    )(near(landed))
 
 
 def on_device(*operands):

time: 93.2 us -> 83.4 us (0.89)
  Pallas kernels: 16.9 us -> 9.03 us
  blocking collectives: 42.2 us -> 38.3 us
  local copies, waits for them, and re-layouts: 1.02 us -> 3.01 us
    pallas_call x4, Pallas kernels: 15.1 us -> 8.14 us  [the longest x1 3.41 us: whole_heads(): pl.pallas_call(convolve_body, out_shape=pltpu.VMEM((frame, 128), jnp.bflo...]
    all_to_all x3, blocking collectives: 42.2 us -> 38.3 us  [exchange(): lax.all_to_all(blocks, 'seq', split_axis=0, concat_axis=0, tiled=True)]
    unnamed x2 -> x16, local copies, waits for them, and re-layouts: 1.02 us -> 3.01 us
where the time goes in v2:
time: 83.4 us; the launch traced here: 83 us
  blocking collectives  38.3 us (46%)
  waiting for transfers between devices  25 us (30%)
  Pallas kernels  9.03 us (11%)
  starting transfers between devices  7.56 us (9%)
  local copies, waits for them, and re-layouts  3.01 us (4%)
    all_to_all x3, blocking collectives, exchange(): lax.all_to_all(blocks, 'seq', split_axis=0, concat_axis=0, tiled=True)  38.3 us
    all_to_all x1, waiting for transfers between devices, exchange(): lax.all_to_all(blocks, 'seq', split_axis=0, concat_axis=0, tiled=True)  25 us
    all_to_all x1, starting transfers between devices, exchange(): lax.all_to_all(blocks, 'seq', split_axis=0, concat_axis=0, tiled=True)  7.56 us
    pallas_call x1, Pallas kernels, whole_heads(): pl.pallas_call(convolve_body, out_shape=pltpu.VMEM((frame, 128), jnp.bflo...  3.41 us
    unnamed x16, local copies, waits for them, and re-layouts  3.01 us
    pallas_call x1, Pallas kernels, whole_heads(): pl.pallas_call(attend_body, out_shape=pltpu.VMEM((devices, local + 8, C_L...  2.83 us
    pallas_call x1, Pallas kernels, whole_heads(): pl.pallas_call(pack_body, out_shape=pltpu.VMEM((devices, 3, local, span),...  1.78 us
  transfers between devices with their start and end apart: 1, of which 1 were waited for; matrix products, arithmetic and copies ran while one was open for 0% of the time, Pallas kernels for 0%

profile of v2, /device:TPU:0, one launch (start us, length us, event | category | flops | bytes accessed | tf_op | source)
XLA Modules:
  0.0 83.0 jit_solution(16605475991397235034)
XLA Ops:
  0.0 0.0 copy-start.3
  0.0 1.0 %copy-done.3 = bf16[48,4096]{1,0:T(8,128)(2,1)S(1)} copy-done((bf16[48,4096]{1,0:T(8,128)(2,1)S(1)}, bf16[48,4096]{1,0:T(8,128)(2,1)}, u32[]{:S(2)}) %copy-start.3) | copy-done | bytes 393240
  1.0 0.0 copy-start.4
  1.0 1.0 %copy-done.4 = bf16[48,4096]{1,0:T(8,128)(2,1)S(1)} copy-done((bf16[48,4096]{1,0:T(8,128)(2,1)S(1)}, bf16[48,4096]{1,0:T(8,128)(2,1)}, u32[]{:S(2)}) %copy-start.4) | copy-done | bytes 393240
  2.0 0.0 copy-start.5
  2.0 1.0 %copy-done.5 = bf16[48,4096]{1,0:T(8,128)(2,1)S(1)} copy-done((bf16[48,4096]{1,0:T(8,128)(2,1)S(1)}, bf16[48,4096]{1,0:T(8,128)(2,1)}, u32[]{:S(2)}) %copy-start.5) | copy-done | bytes 393240
  3.0 1.8 %pack.1 = bf16[16,3,48,256]{3,2,1,0:T(8,128)(2,1)} custom-call(bf16[48,4096]{1,0:T(8,128)(2,1)S(1)} %copy-done.3, bf16[48,4096]{1,0:T(8,128)(2,1)S(1)} %copy-done.4, bf16[48,4096]{1,0:T(8,128)(2,1)S(1)} %copy-done.5), custom_call_target="tpu_custom_call" | custom-call | tf_op jit(solution)/shard_map/pack/pallas_call | solution.py:332
  4.8 0.0 copy-start.1
  4.8 0.0 copy-start.2
  4.8 7.6 %all-to-all-start = ((bf16[16,3,48,256]{3,2,1,0:T(8,128)(2,1)}), bf16[16,3,48,256]{3,2,1,0:T(8,128)(2,1)S(1)}, u32[]{:S(2)}, u32[]{:S(2)}) async-start(bf16[16,3,48,256]{3,2,1,0:T(8,128)(2,1)} %pack.1), calls=%async_computation | async-start | bytes 2359296 | tf_op jit(solution)/shard_map/all_to_all | solution.py:319
  12.4 25.0 %all-to-all-done.rows_ref = bf16[16,3,48,256]{3,2,1,0:T(8,128)(2,1)S(1)} async-done(((bf16[16,3,48,256]{3,2,1,0:T(8,128)(2,1)}), bf16[16,3,48,256]{3,2,1,0:T(8,128)(2,1)S(1)}, u32[]{:S(2)}, u32[]{:S(2)}) %all-to-all-start) | async-done | bytes 1179680 | tf_op jit(solution)/shard_map/all_to_all | solution.py:319
  37.4 0.0 copy-done.1
  37.4 0.0 copy-start
  37.4 2.8 %attend.1 = bf16[16,56,128]{2,1,0:T(8,128)(2,1)S(1)} custom-call(s32[1]{0:T(128)} %bitcast.rank_ref, bf16[16,3,48,256]{3,2,1,0:T(8,128)(2,1)S(1)} %all-to-all-done.rows_ref, bf16[4096,128]{1,0:T(8,128)(2,1)S(1)} %copy-done.1), custom_call_target="tpu_custom_call" | custom-call | tf_op jit(solution)/shard_map/attend/pallas_call | solution.py:342
  40.2 0.0 copy-start.6
  40.3 0.0 copy-start.7
  40.3 16.7 %all_to_all.20.parts_ref = bf16[16,56,128]{2,1,0:T(8,128)(2,1)S(1)} all-to-all(bf16[16,56,128]{2,1,0:T(8,128)(2,1)S(1)} %attend.1), channel_id=1, replica_groups=mesh['groups'=2,'seq'=16] {'seq'}, dimensions={0} | all-to-all | bytes 458752 | tf_op jit(solution)/shard_map/all_to_all | solution.py:319
  57.0 0.1 latents.1
  57.1 11.6 %all_to_all.21 = bf16[16,48,128]{2,1,0:T(8,128)(2,1)S(1)} all-to-all(bf16[16,48,128]{2,1,0:T(8,128)(2,1)S(1)} %latents.1), channel_id=1, replica_groups=mesh['groups'=2,'seq'=16] {'seq'}, dimensions={0} | all-to-all | bytes 393216 | tf_op jit(solution)/shard_map/all_to_all | solution.py:319
  68.7 0.0 copy-done.2
  68.7 0.0 copy-done
  68.7 0.0 copy-done.6
  68.7 0.0 copy-done.7
  68.7 3.4 %convolve.1 = bf16[384,128]{1,0:T(8,128)(2,1)S(1)} custom-call(s32[1]{0:T(128)} %bitcast.rank_ref, bf16[768,128]{1,0:T(8,128)(2,1)S(1)} %bitcast.12, bf16[3456,512]{1,0:T(8,128)(2,1)S(1)} %bitcast.10, f32[1,512]{1,0:T(1,128)S(1)} %bitcast.15, bf16[3,288,512]{2,1,0:T(8,128)(2,1)S(1)} %bitcast.11, f32[1,512]{1,0:T(1,128)S(1)} %bitcast.16), custom_call_target="tpu_custom_call" | custom-call | tf_op jit(solution)/shard_map/convolve/pallas_call | solution.py:361
  72.1 10.0 %all_to_all.22 = bf16[16,24,128]{2,1,0:T(8,128)(2,1)S(1)} all-to-all(bf16[16,24,128]{2,1,0:T(8,128)(2,1)S(1)} %bitcast.14), channel_id=1, replica_groups=mesh['groups'=2,'seq'=16] {'seq'}, dimensions={0} | all-to-all | bytes 196608 | tf_op jit(solution)/shard_map/all_to_all | solution.py:319
  82.1 0.9 %shuffle.1 = bf16[1,2,2,48,128]{4,3,2,1,0:T(8,128)(2,1)} custom-call(bf16[384,128]{1,0:T(8,128)(2,1)S(1)} %bitcast.13), custom_call_target="tpu_custom_call" | custom-call | tf_op jit(solution)/shard_map/shuffle/pallas_call | solution.py:378
Async XLA Ops:
  0.0 1.0 %copy-start.3 = (bf16[48,4096]{1,0:T(8,128)(2,1)S(1)}, bf16[48,4096]{1,0:T(8,128)(2,1)}, u32[]{:S(2)}) copy-start(bf16[48,4096]{1,0:T(8,128)(2,1)} %query_ref.1) | copy-start | bytes 1179652
  1.0 1.0 %copy-start.4 = (bf16[48,4096]{1,0:T(8,128)(2,1)S(1)}, bf16[48,4096]{1,0:T(8,128)(2,1)}, u32[]{:S(2)}) copy-start(bf16[48,4096]{1,0:T(8,128)(2,1)} %key_ref.1) | copy-start | bytes 1179652
  2.0 1.0 %copy-start.5 = (bf16[48,4096]{1,0:T(8,128)(2,1)S(1)}, bf16[48,4096]{1,0:T(8,128)(2,1)}, u32[]{:S(2)}) copy-start(bf16[48,4096]{1,0:T(8,128)(2,1)} %value_ref.1) | copy-start | bytes 1179652
  4.8 32.6 %copy-start.1 = (bf16[4096,128]{1,0:T(8,128)(2,1)S(1)}, bf16[4096,128]{1,0:T(8,128)(2,1)}, u32[]{:S(2)}) copy-start(bf16[4096,128]{1,0:T(8,128)(2,1)} %proj_ref.1) | copy-start | bytes 3145732
  4.8 63.9 %copy-start.2 = (bf16[3,3,3,512,32]{3,4,2,1,0:T(8,128)(2,1)S(1)}, bf16[3,3,3,512,32]{3,4,2,1,0:T(8,128)(2,1)}, u32[]{:S(2)}) copy-start(bf16[3,3,3,512,32]{3,4,2,1,0:T(8,128)(2,1)} %param.14) | copy-start | bytes 2654212
  4.8 32.6 %all-to-all-start = ((bf16[16,3,48,256]{3,2,1,0:T(8,128)(2,1)}), bf16[16,3,48,256]{3,2,1,0:T(8,128)(2,1)S(1)}, u32[]{:S(2)}, u32[]{:S(2)}) async-start(bf16[16,3,48,256]{3,2,1,0:T(8,128)(2,1)} %pack.1), calls=%async_computation | async-start | bytes 2359296 | tf_op jit(solution)/shard_map/all_to_all | solution.py:319
  37.4 31.3 %copy-start = (bf16[3,3,3,128,512]{4,3,2,1,0:T(8,128)(2,1)S(1)}, bf16[3,3,3,128,512]{4,3,2,1,0:T(8,128)(2,1)}, u32[]{:S(2)}) copy-start(bf16[3,3,3,128,512]{4,3,2,1,0:T(8,128)(2,1)} %param.12) | copy-start | bytes 10616836
  40.2 28.4 %copy-start.6 = (f32[512]{0:T(512)S(1)}, f32[512]{0:T(512)}, u32[]{:S(2)}) copy-start(f32[512]{0:T(512)} %param.13) | copy-start | bytes 6148
  40.3 28.4 %copy-start.7 = (f32[512]{0:T(512)S(1)}, f32[512]{0:T(512)}, u32[]{:S(2)}) copy-start(f32[512]{0:T(512)} %param.15) | copy-start | bytes 6148
